TPU v7x, 32 devices: a whole 2x2x4 slice. The times are simulated.
32 devices in a mesh: groups: 2 (over y), tok: 4 (over z), mod: 2 (over x), fsdp: 2 (over core).
Axes of the slice: x: 2, y: 2, z: 4, core: 2. Of those that a mesh axis runs over, the one named last changes fastest.
Arguments:
- residual: bfloat16 [1024, 4096], P(('groups', 'tok'), ('fsdp', 'mod')), parts along dimension 0, may hold values from -30 to 30
- context: bfloat16 [1024, 4096], P(('groups', 'tok'), ('mod', 'fsdp')), parts along dimension 0, may hold values from -6 to 6
- out_proj: bfloat16 [4096, 4096], P('tok', ('fsdp', 'mod')), may hold values from -0.09375 to 0.09375
- norm_gain: bfloat16 [2, 4096], P(None, ('fsdp', 'mod')), may hold values from 0.099609375 to 1.8984375
- router_weight: bfloat16 [4096, 4], P(('fsdp', 'mod')), may hold values from -0.25 to 0.25
- block_modality: int32 [8], P(('groups', 'tok')), parts along dimension 0, may hold values from 0 to 1, as said below
- expert_rows: int32 [4, 128], P(None, ('groups', 'tok')), parts along dimension 1, may hold values from -1 to 127, as said below
- gate_weight: bfloat16 [4, 4096, 11008], P('mod', 'fsdp', 'tok'), may hold values from -0.09375 to 0.09375
- up_weight: bfloat16 [4, 4096, 11008], P('mod', 'fsdp', 'tok'), may hold values from -0.09375 to 0.09375
- down_weight: bfloat16 [4, 11008, 4096], P('mod', 'tok', 'fsdp'), may hold values from -0.0546875 to 0.0546875
Outputs:
- expert_out: bfloat16 [1024, 4096], P(('groups', 'tok'), ('fsdp', 'mod')), parts along dimension 0
There are 2 independent parts, one for each index of `groups`. A program takes and returns all parts, laid end to end along the dimension named above; an argument that names none is the same for every part. Nothing has to cross between parts.
Inputs may be any that keep to these rules, and one draw needn't show every extreme that they name: `block_modality`: both modalities occur in every window. `expert_rows`: slot s = t * 16 + j of expert e names a row among tokens t * 128 to (t + 1) * 128 - 1, or is -1 if unused. Experts below 2 take only text tokens, the others only image tokens; no expert takes a token twice; in each aligned block of 16 slots the used ones come first; every expert fills all 16 slots of at least one index of tok whose tokens have the expert's modality.
All inputs are finite; a program needn't handle non-finite values.
Results may differ from a plain program's by a relative error of at most 0.02.
Values may be sent and summed in bfloat16 or wider, within the bound.
No kernel may reach another device: no remote copies, remote signals or barrier semaphores. Data moves between devices by JAX's collectives and lax.ppermute only.
A program may use at most 192 MiB of HBM per device.

v0:
```python
import jax
import jax.numpy as jnp
from jax import lax
from jax.sharding import PartitionSpec as P

D = 4096
BLOCK = 128


def local(
    residual,
    context,
    out_proj,
    norm_gain,
    router_weight,
    block_modality,
    expert_rows,
    gate_weight,
    up_weight,
    down_weight,
):
    full_context = lax.all_gather(context, ("mod", "fsdp"), axis=1, tiled=True)
    token_count = residual.shape[0]
    projected = jnp.dot(
        full_context,
        lax.all_gather(out_proj, "tok", axis=0, tiled=True),
        preferred_element_type=jnp.float32,
    )
    hidden = residual.astype(jnp.float32) + projected
    token_mod = jnp.repeat(block_modality, BLOCK)
    gain_table = norm_gain.astype(jnp.float32)
    token_gain = jnp.where(token_mod[:, None] == 0, gain_table[0][None, :], gain_table[1][None, :])
    gained = hidden * token_gain
    router_table = router_weight.astype(jnp.float32)
    squares = jnp.sum(hidden * hidden, axis=1)
    square_total = lax.psum(squares, ("mod", "fsdp"))
    inverse = lax.rsqrt(square_total / D + 1e-05)
    normed = gained * inverse[:, None]
    logits = lax.psum(
        jnp.dot(normed, router_table, precision=lax.Precision.HIGHEST), ("mod", "fsdp")
    )
    score = jax.nn.sigmoid(logits)
    normed_rows = normed.astype(jnp.bfloat16)
    local_experts = gate_weight.shape[0]
    first_expert = lax.axis_index("mod") * local_experts
    row_ids = lax.iota(jnp.int32, token_count)
    own_rows = lax.dynamic_slice_in_dim(expert_rows, first_expert, local_experts, 0)
    own_pick = (own_rows[:, :, None] == row_ids[None, None, :]).astype(jnp.bfloat16)
    half_rows = lax.all_gather(normed_rows, "mod", axis=1, tiled=True)
    chosen = jnp.einsum(
        "ecr,rd->ecd", own_pick, half_rows, preferred_element_type=jnp.float32
    ).astype(jnp.bfloat16)
    unit_count = gate_weight.shape[2]
    piece = lax.all_gather(chosen, "tok", axis=1, tiled=True)
    gate_part = jnp.einsum("esd,edf->esf", piece, gate_weight, preferred_element_type=jnp.float32)
    up_part = jnp.einsum("esd,edf->esf", piece, up_weight, preferred_element_type=jnp.float32)
    partial_in = jnp.concatenate((gate_part, up_part), axis=2)
    summed_in = lax.psum(partial_in.astype(jnp.bfloat16), "fsdp").astype(jnp.float32)
    activation = (jax.nn.silu(summed_in[:, :, :unit_count]) * summed_in[:, :, unit_count:]).astype(
        jnp.bfloat16
    )
    expert_value = lax.psum_scatter(
        jnp.einsum(
            "esf,efd->sed", activation, down_weight, preferred_element_type=jnp.float32
        ).astype(jnp.bfloat16),
        "tok",
        scatter_dimension=0,
        tiled=True,
    ).astype(jnp.float32)
    own_score = lax.dynamic_slice_in_dim(score, first_expert, local_experts, 1)
    pick_table = own_pick.astype(jnp.float32)
    slot_score = jnp.einsum("ecr,re->ce", pick_table, own_score, precision=lax.Precision.HIGHEST)
    scaled = expert_value * slot_score[:, :, None]
    mixed_rows = jnp.einsum("ecr,ced->rd", pick_table, scaled, precision=lax.Precision.HIGHEST)
    combined = lax.psum_scatter(
        mixed_rows.astype(jnp.bfloat16), "mod", scatter_dimension=1, tiled=True
    )
    return combined


def solution(mesh):
    placed = (
        P(("groups", "tok"), ("fsdp", "mod")),
        P(("groups", "tok"), ("mod", "fsdp")),
        P("tok", ("fsdp", "mod")),
        P(None, ("fsdp", "mod")),
        P(("fsdp", "mod"), None),
        P(("groups", "tok")),
        P(None, ("groups", "tok")),
        P("mod", "fsdp", "tok"),
        P("mod", "fsdp", "tok"),
        P("mod", "tok", "fsdp"),
    )
    return jax.shard_map(
        local,
        mesh=mesh,
        in_specs=placed,
        out_specs=P(("groups", "tok"), ("fsdp", "mod")),
        check_vma=False,
    )
```

profile of v0, /device:TPU:0, one launch (start us, length us, event | category | flops | bytes accessed | tf_op | source)
XLA Modules:
  0.0 316.3 jit_solution(1377281258367514044)
XLA Ops:
  6.5 0.0 copy-start
  6.5 0.7 all-gather.3.cloned.1.call-update
  7.3 0.0 all-gather.5.cloned.1.call-start
  7.3 0.7 all-gather.5.cloned.1.call-update
  8.0 0.0 all-reduce.2.cloned.1.call-start
  8.7 0.7 convert_element_type.35
  9.4 0.7 constant_dynamic-slice_fusion.1
  10.1 18.3 %all-gather.3.cloned.1.call-done = bf16[128,4096]{1,0:T(8,128)(2,1)} async-done(((bf16[128,1024]{1,0:T(8,128)(2,1)}), bf16[128,4096]{1,0:T(8,128)(2,1)}) %all-gather.3.cloned.1.call-update) | async-done | bytes 1048592 | tf_op jit(solution)/shard_map/all_gather | solution.py:22
  28.4 151.2 %all-gather.5.cloned.1.call-done = bf16[4096,1024]{1,0:T(8,128)(2,1)} async-done(((bf16[1024,1024]{1,0:T(8,128)(2,1)}), bf16[4096,1024]{1,0:T(8,128)(2,1)}) %all-gather.5.cloned.1.call-update) | async-done | bytes 8388624 | tf_op jit(solution)/shard_map/all_gather | solution.py:26
  179.6 5.0 %multiply_reduce_fusion = (f32[128]{0:T(128)S(1)}, f32[128,1024]{1,0:T(8,128)S(1)}) fusion(bf16[128,4096]{1,0:T(8,128)(2,1)} %all-gather.3.cloned.1.call-done, bf16[4096,1024]{1,0:T(8,128)(2,1)} %all-gather.5.cloned.1.call-done, bf16[128,1024]{1,0:T(8,128)(2,1)} %param.10), kind=kOutput, calls=%fused_computation.13 | convolution fusion | flops 1074265984 | bytes 10224128 | tf_op jit(solution)/shard_map/dot_general | solution.py:24
  184.6 6.8 %psum.21 = f32[128]{0:T(128)S(1)} all-reduce(f32[128]{0:T(128)S(1)} %get-tuple-element.5), channel_id=1, replica_groups=mesh['groups'=2,'tok'=4,'mod'=2,'fsdp'=2] {'mod','fsdp'}, use_global_device_ids=true, to_apply=%region_1.2 | all-reduce | flops 128 | bytes 1024 | tf_op jit(solution)/shard_map/psum | solution.py:36
  191.5 0.1 fusion.7
  191.6 7.6 %all_gather.14 = bf16[128,2048]{1,0:T(8,128)(2,1)S(1)} all-gather(bf16[128,1024]{1,0:T(8,128)(2,1)S(1)} %fusion.7), channel_id=1, replica_groups=mesh['groups'=2,'tok'=4,'mod'=2,'fsdp'=2] {'mod'}, dimensions={1}, use_global_device_ids=true | all-gather | bytes 786432 | tf_op jit(solution)/shard_map/all_gather | solution.py:49
  199.1 0.2 convolution_convert_fusion.3
  199.4 14.7 %all_gather.15 = bf16[2,64,2048]{2,1,0:T(8,128)(2,1)S(1)} all-gather(bf16[2,16,2048]{2,1,0:T(8,128)(2,1)S(1)} %convolution_convert_fusion.3), channel_id=1, replica_groups=mesh['groups'=2,'tok'=4,'mod'=2,'fsdp'=2] {'tok'}, dimensions={1}, use_global_device_ids=true | all-gather | bytes 655360 | tf_op jit(solution)/shard_map/all_gather | solution.py:54
  214.1 11.3 %convolution_convert_fusion = bf16[2,64,2752]{2,1,0:T(8,128)(2,1)S(1)} fusion(bf16[2,64,2048]{2,1,0:T(8,128)(2,1)S(1)} %all_gather.15, bf16[2,2048,2752]{1,2,0:T(8,128)(2,1)} %param.18), kind=kOutput, calls=%fused_computation | convolution fusion | flops 1443192832 | bytes 23773184 | tf_op jit(solution)/shard_map/esd,edf->esf/dot_general | solution.py:56
  225.4 11.3 %convolution_convert_fusion.1 = bf16[2,64,2752]{2,1,0:T(8,128)(2,1)S(1)} fusion(bf16[2,64,2048]{2,1,0:T(8,128)(2,1)S(1)} %all_gather.15, bf16[2,2048,2752]{1,2,0:T(8,128)(2,1)} %param.17), kind=kOutput, calls=%fused_computation.1 | convolution fusion | flops 1443192832 | bytes 23773184 | tf_op jit(solution)/shard_map/esd,edf->esf/dot_general | solution.py:55
  236.7 1.4 pad_maximum_fusion
  238.1 0.0 all-reduce.2.cloned.1.call-update
  238.1 0.0 reduce-scatter.3.cloned.1.call-start
  238.2 19.4 %all-reduce.2.cloned.1.call-done = bf16[2,64,5504]{2,1,0:T(8,128)(2,1)} async-done(((bf16[2,64,5504]{2,1,0:T(8,128)(2,1)}), bf16[2,64,5504]{2,1,0:T(8,128)(2,1)}) %all-reduce.2.cloned.1.call-update) | async-done | bytes 1409040 | tf_op jit(solution)/shard_map/psum | solution.py:58
  257.6 1.5 convert_element_type.38
  259.1 12.3 %fusion.1 = bf16[64,2,2048]{2,0,1:T(8,128)(2,1)} fusion(bf16[2,2752,2048]{2,1,0:T(8,128)(2,1)} %param.19, f32[2,64,5504]{2,1,0:T(8,128)S(1)} %convert_element_type.38), kind=kOutput, calls=%fused_computation.5 | convolution fusion | flops 1445216256 | bytes 25952256 | tf_op jit(solution)/shard_map/esf,efd->sed/dot_general | solution.py:63
  271.4 0.0 reduce-scatter.3.cloned.1.call-update
  271.4 0.0 reduce-scatter.5.cloned.1.call-start
  271.5 0.4 fusion.6
  271.9 7.3 %psum.23 = f32[128,4]{0,1:T(4,128)S(1)} all-reduce(f32[128,4]{0,1:T(4,128)S(1)} %fusion.6), channel_id=1, replica_groups=mesh['groups'=2,'tok'=4,'mod'=2,'fsdp'=2] {'mod','fsdp'}, use_global_device_ids=true, to_apply=%region_4.5 | all-reduce | flops 512 | bytes 4096 | tf_op jit(solution)/shard_map/psum | solution.py:39
  279.2 0.2 fusion.13
  279.4 15.0 %reduce-scatter.3.cloned.1.call-done = bf16[16,2,2048]{2,0,1:T(8,128)(2,1)} async-done(((bf16[64,2,2048]{2,0,1:T(8,128)(2,1)}), bf16[16,2,2048]{2,0,1:T(8,128)(2,1)}) %reduce-scatter.3.cloned.1.call-update) | async-done | bytes 131088 | tf_op jit(solution)/shard_map/reduce_scatter | solution.py:62
  294.4 2.4 fusion
  296.8 0.0 reduce-scatter.5.cloned.1.call-update
  296.8 12.9 %reduce-scatter.5.cloned.1.call-done = bf16[128,1024]{1,0:T(8,128)(2,1)} async-done(((bf16[128,2048]{1,0:T(8,128)(2,1)}), bf16[128,1024]{1,0:T(8,128)(2,1)}) %reduce-scatter.5.cloned.1.call-update) | async-done | bytes 262160 | tf_op jit(solution)/shard_map/reduce_scatter | solution.py:75
  (6 shorter events, 0.0 us)
Async XLA Ops:
  6.5 264.9 %copy-start = (bf16[1024,4]{0,1:T(4,128)(2,1)S(1)}, bf16[1024,4]{0,1:T(4,128)(2,1)}, u32[]{:S(2)}) copy-start(bf16[1024,4]{0,1:T(4,128)(2,1)} %param.14) | copy-start | bytes 24580
  6.5 21.8 %all-gather.3.cloned.1.call-start = ((), (), s32[]{:S(2)}) async-start(), calls=%async_computation.2 | async-start | bytes 1310720 | tf_op jit(solution)/shard_map/all_gather | solution.py:22
  7.3 172.4 %all-gather.5.cloned.1.call-start = ((), (), s32[]{:S(2)}) async-start(), calls=%async_computation.3 | async-start | bytes 10485760 | tf_op jit(solution)/shard_map/all_gather | solution.py:26
  8.0 249.5 %all-reduce.2.cloned.1.call-start = ((), (), s32[]{:S(2)}) async-start(), calls=%async_computation.4 | async-start | bytes 2818048 | tf_op jit(solution)/shard_map/psum | solution.py:58
  238.1 56.3 %reduce-scatter.3.cloned.1.call-start = ((), (), s32[]{:S(2)}) async-start(), calls=%async_computation.5 | async-start | bytes 655360 | tf_op jit(solution)/shard_map/reduce_scatter | solution.py:62
  271.4 38.4 %reduce-scatter.5.cloned.1.call-start = ((), (), s32[]{:S(2)}) async-start(), calls=%async_computation.6 | async-start | bytes 786432 | tf_op jit(solution)/shard_map/reduce_scatter | solution.py:75
Sparse Core Ops, SparseCore 0:
  8.9 19.4 all-gather.2
  29.9 149.6 all-gather.4
  238.2 19.2 all-reduce.1
  271.5 22.8 reduce-scatter.2
  296.9 12.7 reduce-scatter.4
where the time goes:
time: 317 us; the launch traced here: 316 us
  waiting for transfers between devices  218 us (69%)
  matrix products  43.1 us (14%)
  blocking collectives  36.4 us (11%)
  between operations  13.8 us (4%)
  other arithmetic  3.74 us (1%)
    all_gather x1, waiting for transfers between devices, local(): lax.all_gather(out_proj, 'tok', axis=0, tiled=True)  151 us
    psum x1, waiting for transfers between devices, local(): lax.psum(partial_in.astype(jnp.bfloat16), 'fsdp').astype(jnp.float32)  19.4 us
    all_gather x1, waiting for transfers between devices, local(): full_context = lax.all_gather(context, ('mod', 'fsdp'), axis=1, tiled=True)  18.3 us
    reduce_scatter x1, waiting for transfers between devices, local(): lax.psum_scatter(jnp.einsum('esf,efd->sed', activation, down_weight, pref...  15 us
    all_gather x1, blocking collectives, local(): piece = lax.all_gather(chosen, 'tok', axis=1, tiled=True)  14.7 us
    reduce_scatter x1, waiting for transfers between devices, local(): lax.psum_scatter(mixed_rows.astype(jnp.bfloat16), 'mod', scatter_dimensio...  12.9 us
    dot_general x1, matrix products, local(): jnp.einsum('esf,efd->sed', activation, down_weight, preferred_element_typ...  12.3 us
    dot_general x1, matrix products, local(): jnp.einsum('esd,edf->esf', piece, gate_weight, preferred_element_type=jnp...  11.3 us
  transfers between devices with their start and end apart: 5, of which 5 were waited for; matrix products, arithmetic and copies ran while one was open for 1% of the time, Pallas kernels for 0%

commit v1 on v0

--- a/solution.py
+++ b/solution.py
@@ -2,6 +2,7 @@
 import jax.numpy as jnp
 from jax import lax
 from jax.sharding import PartitionSpec as P
+from jax.lax import all_gather
 
 D = 4096
 BLOCK = 128
@@ -36,9 +37,8 @@
     square_total = lax.psum(squares, ("mod", "fsdp"))
     inverse = lax.rsqrt(square_total / D + 1e-05)
     normed = gained * inverse[:, None]
-    logits = lax.psum(
-        jnp.dot(normed, router_table, precision=lax.Precision.HIGHEST), ("mod", "fsdp")
-    )
+    chunk = jnp.dot(normed, router_table, precision=lax.Precision.HIGHEST)
+    logits = jnp.sum(all_gather(chunk, ("mod", "fsdp")), axis=0)
     score = jax.nn.sigmoid(logits)
     normed_rows = normed.astype(jnp.bfloat16)
     local_experts = gate_weight.shape[0]

time: 317 us -> 317 us (level)
    psum x1 -> x0, blocking collectives: 7.27 us -> none  [local(): lax.psum(jnp.dot(normed, router_table, precision=lax.Precision.HIGHEST),...]
    all_gather x0 -> x1, blocking collectives: none -> 5.17 us  [local(): logits = jnp.sum(all_gather(chunk, ('mod', 'fsdp')), axis=0)]
where the time goes in v1:
time: 317 us; the launch traced here: 316 us
  waiting for transfers between devices  220 us (69%)
  matrix products  43.1 us (14%)
  blocking collectives  34.3 us (11%)
  between operations  13.8 us (4%)
  other arithmetic  3.76 us (1%)
    all_gather x1, waiting for transfers between devices, local(): lax.all_gather(out_proj, 'tok', axis=0, tiled=True)  151 us
    psum x1, waiting for transfers between devices, local(): lax.psum(partial_in.astype(jnp.bfloat16), 'fsdp').astype(jnp.float32)  19.4 us
    all_gather x1, waiting for transfers between devices, local(): full_context = lax.all_gather(context, ('mod', 'fsdp'), axis=1, tiled=True)  18.3 us
    reduce_scatter x1, waiting for transfers between devices, local(): lax.psum_scatter(jnp.einsum('esf,efd->sed', activation, down_weight, pref...  17.1 us
    all_gather x1, blocking collectives, local(): piece = lax.all_gather(chosen, 'tok', axis=1, tiled=True)  14.7 us
    reduce_scatter x1, waiting for transfers between devices, local(): lax.psum_scatter(mixed_rows.astype(jnp.bfloat16), 'mod', scatter_dimensio...  12.9 us
    dot_general x1, matrix products, local(): jnp.einsum('esf,efd->sed', activation, down_weight, preferred_element_typ...  12.3 us
    dot_general x1, matrix products, local(): jnp.einsum('esd,edf->esf', piece, gate_weight, preferred_element_type=jnp...  11.3 us
  transfers between devices with their start and end apart: 5, of which 5 were waited for; matrix products, arithmetic and copies ran while one was open for 1% of the time, Pallas kernels for 0%

profile of v1, /device:TPU:0, one launch (start us, length us, event | category | flops | bytes accessed | tf_op | source)
XLA Modules:
  0.0 316.3 jit_solution(40605309758779995)
XLA Ops:
  6.5 0.0 copy-start
  6.5 0.7 all-gather.4.cloned.1.call-update
  7.3 0.0 all-gather.6.cloned.1.call-start
  7.3 0.7 all-gather.6.cloned.1.call-update
  8.0 0.0 all-reduce.2.cloned.1.call-start
  8.7 0.7 convert_element_type.35
  9.4 0.7 constant_dynamic-slice_fusion.1
  10.1 18.3 %all-gather.4.cloned.1.call-done = bf16[128,4096]{1,0:T(8,128)(2,1)} async-done(((bf16[128,1024]{1,0:T(8,128)(2,1)}), bf16[128,4096]{1,0:T(8,128)(2,1)}) %all-gather.4.cloned.1.call-update) | async-done | bytes 1048592 | tf_op jit(solution)/shard_map/all_gather | solution.py:23
  28.4 151.2 %all-gather.6.cloned.1.call-done = bf16[4096,1024]{1,0:T(8,128)(2,1)} async-done(((bf16[1024,1024]{1,0:T(8,128)(2,1)}), bf16[4096,1024]{1,0:T(8,128)(2,1)}) %all-gather.6.cloned.1.call-update) | async-done | bytes 8388624 | tf_op jit(solution)/shard_map/all_gather | solution.py:27
  179.6 5.0 %multiply_reduce_fusion = (f32[128]{0:T(128)S(1)}, f32[128,1024]{1,0:T(8,128)S(1)}) fusion(bf16[128,4096]{1,0:T(8,128)(2,1)} %all-gather.4.cloned.1.call-done, bf16[4096,1024]{1,0:T(8,128)(2,1)} %all-gather.6.cloned.1.call-done, bf16[128,1024]{1,0:T(8,128)(2,1)} %param.10), kind=kOutput, calls=%fused_computation.13 | convolution fusion | flops 1074265984 | bytes 10224128 | tf_op jit(solution)/shard_map/dot_general | solution.py:25
  184.6 6.8 %psum.14 = f32[128]{0:T(128)S(1)} all-reduce(f32[128]{0:T(128)S(1)} %get-tuple-element.5), channel_id=1, replica_groups=mesh['groups'=2,'tok'=4,'mod'=2,'fsdp'=2] {'mod','fsdp'}, use_global_device_ids=true, to_apply=%region_1.2 | all-reduce | flops 128 | bytes 1024 | tf_op jit(solution)/shard_map/psum | solution.py:37
  191.5 0.1 fusion.7
  191.6 7.6 %all_gather.20 = bf16[128,2048]{1,0:T(8,128)(2,1)S(1)} all-gather(bf16[128,1024]{1,0:T(8,128)(2,1)S(1)} %fusion.7), channel_id=1, replica_groups=mesh['groups'=2,'tok'=4,'mod'=2,'fsdp'=2] {'mod'}, dimensions={1}, use_global_device_ids=true | all-gather | bytes 786432 | tf_op jit(solution)/shard_map/all_gather | solution.py:49
  199.1 0.2 convolution_convert_fusion.3
  199.4 14.7 %all_gather.21 = bf16[2,64,2048]{2,1,0:T(8,128)(2,1)S(1)} all-gather(bf16[2,16,2048]{2,1,0:T(8,128)(2,1)S(1)} %convolution_convert_fusion.3), channel_id=1, replica_groups=mesh['groups'=2,'tok'=4,'mod'=2,'fsdp'=2] {'tok'}, dimensions={1}, use_global_device_ids=true | all-gather | bytes 655360 | tf_op jit(solution)/shard_map/all_gather | solution.py:54
  214.1 11.3 %convolution_convert_fusion = bf16[2,64,2752]{2,1,0:T(8,128)(2,1)S(1)} fusion(bf16[2,64,2048]{2,1,0:T(8,128)(2,1)S(1)} %all_gather.21, bf16[2,2048,2752]{1,2,0:T(8,128)(2,1)} %param.18), kind=kOutput, calls=%fused_computation | convolution fusion | flops 1443192832 | bytes 23773184 | tf_op jit(solution)/shard_map/esd,edf->esf/dot_general | solution.py:56
  225.4 11.3 %convolution_convert_fusion.1 = bf16[2,64,2752]{2,1,0:T(8,128)(2,1)S(1)} fusion(bf16[2,64,2048]{2,1,0:T(8,128)(2,1)S(1)} %all_gather.21, bf16[2,2048,2752]{1,2,0:T(8,128)(2,1)} %param.17), kind=kOutput, calls=%fused_computation.1 | convolution fusion | flops 1443192832 | bytes 23773184 | tf_op jit(solution)/shard_map/esd,edf->esf/dot_general | solution.py:55
  236.7 1.4 pad_maximum_fusion
  238.1 0.0 all-reduce.2.cloned.1.call-update
  238.1 0.0 reduce-scatter.3.cloned.1.call-start
  238.2 19.4 %all-reduce.2.cloned.1.call-done = bf16[2,64,5504]{2,1,0:T(8,128)(2,1)} async-done(((bf16[2,64,5504]{2,1,0:T(8,128)(2,1)}), bf16[2,64,5504]{2,1,0:T(8,128)(2,1)}) %all-reduce.2.cloned.1.call-update) | async-done | bytes 1409040 | tf_op jit(solution)/shard_map/psum | solution.py:58
  257.6 1.5 convert_element_type.38
  259.1 12.3 %fusion.1 = bf16[64,2,2048]{2,0,1:T(8,128)(2,1)} fusion(bf16[2,2752,2048]{2,1,0:T(8,128)(2,1)} %param.19, f32[2,64,5504]{2,1,0:T(8,128)S(1)} %convert_element_type.38), kind=kOutput, calls=%fused_computation.5 | convolution fusion | flops 1445216256 | bytes 25952256 | tf_op jit(solution)/shard_map/esf,efd->sed/dot_general | solution.py:63
  271.4 0.0 reduce-scatter.3.cloned.1.call-update
  271.4 0.0 reduce-scatter.5.cloned.1.call-start
  271.5 0.4 fusion.6
  271.9 5.2 %all-gather = f32[512,4]{0,1:T(4,128)S(1)} all-gather(f32[128,4]{0,1:T(4,128)S(1)} %fusion.6), channel_id=2, replica_groups=mesh['groups'=2,'tok'=4,'mod'=2,'fsdp'=2] {'mod','fsdp'}, dimensions={0}, use_global_device_ids=true | all-gather | bytes 10240 | tf_op jit(solution)/shard_map/all_gather | solution.py:41
  277.1 0.2 fusion.13
  277.3 17.1 %reduce-scatter.3.cloned.1.call-done = bf16[16,2,2048]{2,0,1:T(8,128)(2,1)} async-done(((bf16[64,2,2048]{2,0,1:T(8,128)(2,1)}), bf16[16,2,2048]{2,0,1:T(8,128)(2,1)}) %reduce-scatter.3.cloned.1.call-update) | async-done | bytes 131088 | tf_op jit(solution)/shard_map/reduce_scatter | solution.py:62
  294.4 2.4 fusion
  296.8 0.0 reduce-scatter.5.cloned.1.call-update
  296.8 12.9 %reduce-scatter.5.cloned.1.call-done = bf16[128,1024]{1,0:T(8,128)(2,1)} async-done(((bf16[128,2048]{1,0:T(8,128)(2,1)}), bf16[128,1024]{1,0:T(8,128)(2,1)}) %reduce-scatter.5.cloned.1.call-update) | async-done | bytes 262160 | tf_op jit(solution)/shard_map/reduce_scatter | solution.py:75
  (8 shorter events, 0.1 us)
Async XLA Ops:
  6.5 264.9 %copy-start = (bf16[1024,4]{0,1:T(4,128)(2,1)S(1)}, bf16[1024,4]{0,1:T(4,128)(2,1)}, u32[]{:S(2)}) copy-start(bf16[1024,4]{0,1:T(4,128)(2,1)} %param.14) | copy-start | bytes 24580
  6.5 21.8 %all-gather.4.cloned.1.call-start = ((), (), s32[]{:S(2)}) async-start(), calls=%async_computation.2 | async-start | bytes 1310720 | tf_op jit(solution)/shard_map/all_gather | solution.py:23
  7.3 172.4 %all-gather.6.cloned.1.call-start = ((), (), s32[]{:S(2)}) async-start(), calls=%async_computation.3 | async-start | bytes 10485760 | tf_op jit(solution)/shard_map/all_gather | solution.py:27
  8.0 249.5 %all-reduce.2.cloned.1.call-start = ((), (), s32[]{:S(2)}) async-start(), calls=%async_computation.4 | async-start | bytes 2818048 | tf_op jit(solution)/shard_map/psum | solution.py:58
  238.1 56.3 %reduce-scatter.3.cloned.1.call-start = ((), (), s32[]{:S(2)}) async-start(), calls=%async_computation.5 | async-start | bytes 655360 | tf_op jit(solution)/shard_map/reduce_scatter | solution.py:62
  271.4 38.4 %reduce-scatter.5.cloned.1.call-start = ((), (), s32[]{:S(2)}) async-start(), calls=%async_computation.6 | async-start | bytes 786432 | tf_op jit(solution)/shard_map/reduce_scatter | solution.py:75
Sparse Core Ops, SparseCore 0:
  8.9 19.4 all-gather.3
  29.9 149.6 all-gather.5
  238.2 19.2 all-reduce.1
  271.5 22.8 reduce-scatter.2
  296.9 12.7 reduce-scatter.4
